TPU v7x, 512 devices: a whole 4x8x8 slice. The times are simulated.
512 devices in a mesh: dp: 64 (over z, x, core), expert: 8 (over y).
Axes of the slice: x: 4, y: 8, z: 8, core: 2. Of those that a mesh axis runs over, the one named last changes fastest.
Arguments:
- tokens: bfloat16 [512, 2048], P('dp'), may hold values from -6 to 6
- expert_ids: int32 [512, 2], P('dp'), may hold values from 0 to 15, all different within a row; in each aligned block of 8 rows (0 to 7, 8 to 15, ...) at most 2 rows name the same one
- gate_levels: int32 [512, 2], P('dp'), may hold values from 1 to 1023
- w_gate: bfloat16 [16, 2048, 8192], P('expert', None, 'dp'), may hold values from -0.125 to 0.125
- w_up: bfloat16 [16, 2048, 8192], P('expert', None, 'dp'), may hold values from -0.125 to 0.125
- w_down: bfloat16 [16, 8192, 2048], P('expert', 'dp'), may hold values from -0.0625 to 0.0625
Outputs:
- moe_out: bfloat16 [512, 2048], P('dp')
Inputs may be any that keep to these rules, and one draw needn't show every extreme that they name: `expert_ids`: the two experts of a token differ. Among the 8 rows of one index of dp (rows i * 8 to (i + 1) * 8 - 1) no expert is named by more than 2 rows, a bound that some block reaches.
All inputs are finite; a program needn't handle non-finite values.
Results may differ from a plain program's by a relative error of at most 0.0049.
Values may be sent and summed in bfloat16 or wider, within the bound.
A program may use at most 64 MiB of HBM per device.

v0:
```python
import jax
import jax.numpy as jnp
from jax import lax
from jax.sharding import PartitionSpec as P


def route_map(expert_ids, first_expert, n_owned, slots):
    n_rows = expert_ids.shape[0]
    pair_ids = expert_ids.reshape(n_rows * 2)
    owned_ids = jnp.arange(n_owned, dtype=jnp.int32) + first_expert
    matches = (pair_ids[:, None] == owned_ids[None, :]).astype(jnp.int32)
    position = jnp.cumsum(matches, axis=0) - matches
    slot_ids = jnp.arange(slots, dtype=jnp.int32)
    placed = matches[:, None, :] * (position[:, None, :] == slot_ids[None, :, None]).astype(
        jnp.int32
    )
    return placed.reshape(n_rows, 2, slots, n_owned)


def gate_values(gate_levels):
    levels = gate_levels.astype(jnp.float32)
    return levels / jnp.sum(levels, axis=-1, keepdims=True)


def run_experts(row_block, w_gate, w_up, w_down):
    gate_proj = jnp.einsum("rld,ldf->rlf", row_block, w_gate, preferred_element_type=jnp.float32)
    up_proj = jnp.einsum("rld,ldf->rlf", row_block, w_up, preferred_element_type=jnp.float32)
    hidden = (jax.nn.silu(gate_proj) * up_proj).astype(jnp.bfloat16)
    return jnp.einsum("rlf,lfd->rld", hidden, w_down, preferred_element_type=jnp.float32)


def on_device(tokens, expert_ids, gate_levels, w_gate, w_up, w_down):
    n_owned = w_gate.shape[0]
    n_rows = tokens.shape[0]
    width = tokens.shape[1]
    n_experts = n_owned * lax.axis_size("expert")
    slots = 4 * n_rows // n_experts
    first_expert = lax.axis_index("expert") * n_owned
    every_token, every_ids = (
        lax.all_gather(tokens, "dp", axis=0, tiled=True),
        lax.all_gather(expert_ids, "dp", axis=0, tiled=True),
    )
    n_group = every_token.shape[0] // n_rows
    grouped = every_token.reshape(n_group, n_rows, width)
    grouped_ids = every_ids.reshape(n_group, n_rows, 2)
    maps = jax.vmap(lambda ids: route_map(ids, first_expert, n_owned, slots))(grouped_ids)
    selector = jnp.sum(maps, axis=2).astype(jnp.bfloat16)
    buffer = jnp.einsum("nrsl,nrd->nsld", selector, grouped, preferred_element_type=jnp.float32)
    buffer = buffer.astype(jnp.bfloat16).reshape(n_group * slots, n_owned, width)
    route_ids, route_levels = (
        lax.all_gather(expert_ids, "dp", axis=0, tiled=True),
        lax.all_gather(gate_levels, "dp", axis=0, tiled=True),
    )
    n_source = n_rows * lax.axis_size("dp") // n_rows
    outputs = run_experts(buffer, w_gate, w_up, w_down).reshape(n_source, slots, n_owned, width)
    block_ids = route_ids.reshape(n_source, n_rows, 2)
    block_gates = gate_values(route_levels).reshape(n_source, n_rows, 2)
    maps = jax.vmap(lambda ids: route_map(ids, first_expert, n_owned, slots))(block_ids)
    weights = jnp.sum(maps.astype(jnp.float32) * block_gates[:, :, :, None, None], axis=2)
    mixed = jnp.einsum("nrsl,nsld->nrd", weights, outputs, precision=lax.Precision.HIGHEST)
    combined = lax.psum_scatter(
        mixed.reshape(n_rows * lax.axis_size("dp"), width), "dp", scatter_dimension=0, tiled=True
    )
    moe_out = lax.psum(combined, "expert").astype(jnp.bfloat16)
    return moe_out


def solution(mesh):
    in_specs = (
        P("dp", None),
        P("dp", None),
        P("dp", None),
        P("expert", None, "dp"),
        P("expert", None, "dp"),
        P("expert", "dp", None),
    )
    out_specs = P("dp", None)
    return jax.shard_map(
        on_device, mesh=mesh, in_specs=in_specs, out_specs=out_specs, check_vma=False
    )
```

profile of v0, /device:TPU:2, one launch (start us, length us, event | category | flops | bytes accessed | tf_op | source)
XLA Modules:
  0.0 361.0 jit_solution(8371726658748950567)
XLA Ops:
  6.5 0.7 all-gather.4.cloned.1.call-update
  7.3 49.7 %all-gather = s32[64,8,2]{1,2,0:T(2,128)S(1)} all-gather(s32[1,8,2]{1,2,0:T(2,128)} %bitcast.45), channel_id=1, replica_groups=mesh['dp'=64,'expert'=8] {'dp'}, dimensions={0}, use_global_device_ids=true | all-gather | bytes 4160 | tf_op jit(solution)/shard_map/all_gather | solution.py:51
  57.0 0.1 copy.58
  57.0 0.1 copy.60
  57.1 0.2 fusion.7
  57.3 0.2 copy.61
  57.5 0.1 compare_convert_fusion
  57.6 0.1 fusion.20
  57.7 0.1 copy.64
  57.9 41.4 %all-gather.1 = s32[64,8,2]{1,2,0:T(2,128)S(1)} all-gather(s32[1,8,2]{1,2,0:T(2,128)} %bitcast.46), channel_id=1, replica_groups=mesh['dp'=64,'expert'=8] {'dp'}, dimensions={0}, use_global_device_ids=true | all-gather | bytes 4160 | tf_op jit(solution)/shard_map/all_gather | solution.py:52
  99.3 0.1 reshape.48
  99.4 0.1 convert_reduce_fusion
  99.5 0.1 reshape.51
  99.6 0.1 mul.35
  99.8 0.1 copy.67
  99.9 2.5 convolution_convert_fusion
  102.4 2.0 convolution_bitcast_fusion.3
  104.5 2.4 convolution_bitcast_fusion.1
  106.9 2.5 reshape.42
  109.4 7.5 %convolution_bitcast_fusion = f32[512,2048]{1,0:T(8,128)} fusion(f32[64,8,2,2]{1,2,3,0:T(2,128)S(1)} %copy.67, f32[64,2,2,2048]{3,1,0,2:T(2,128)S(1)} %reshape.42), kind=kOutput, calls=%fused_computation | convolution fusion | flops 50331648 | bytes 6299648 | tf_op jit(solution)/shard_map/nrsl,nsld->nrd/dot_general | solution.py:60
  116.9 1.3 dynamic-slice
  118.8 203.7 %all-reduce.3.cloned.1.call-done = f32[512,2048]{1,0:T(8,128)} async-done(((f32[512,2048]{1,0:T(8,128)}), f32[512,2048]{1,0:T(8,128)}) %all-reduce.3.cloned.1.call-update) | async-done | bytes 4194320
  322.5 0.8 constant_dynamic-slice_fusion
  323.4 30.8 %psum.7 = bf16[8,2048]{1,0:T(8,128)(2,1)} all-reduce(f32[8,2048]{1,0:T(8,128)S(1)} %constant_dynamic-slice_fusion), channel_id=1, replica_groups=mesh['dp'=64,'expert'=8] {'expert'}, use_global_device_ids=true, to_apply=%region_5.6 | all-reduce | flops 16384 | bytes 98304 | tf_op jit(solution)/shard_map/psum | solution.py:64
  (16 shorter events, 0.2 us)
Async XLA Ops:
  6.5 97.9 %copy-start = (bf16[2,128,2048]{2,1,0:T(8,128)(2,1)S(1)}, bf16[2,128,2048]{2,1,0:T(8,128)(2,1)}, u32[]{:S(2)}) copy-start(bf16[2,128,2048]{2,1,0:T(8,128)(2,1)} %param.11) | copy-start | bytes 3145732
  6.5 93.4 %all-gather.4.cloned.1.call-start = ((), (), s32[]{:S(2)}) async-start(), calls=%async_computation | async-start | bytes 2129920 | tf_op jit(solution)/shard_map/all_gather | solution.py:40
  7.3 315.3 %all-reduce.3.cloned.1.call-start = ((), (), s32[]{:S(2)}) async-start(), calls=%async_computation.1 | async-start | bytes 8388608
  99.9 4.6 %copy-start.1 = (bf16[2,2048,128]{2,1,0:T(8,128)(2,1)S(1)}, bf16[2,2048,128]{2,1,0:T(8,128)(2,1)}, u32[]{:S(2)}) copy-start(bf16[2,2048,128]{2,1,0:T(8,128)(2,1)} %param.10) | copy-start | bytes 3145732
Sparse Core Ops, SparseCore 0:
  10.7 87.3 all-gather.3
  117.0 205.4 all-reduce.2
where the time goes:
time: 361 us
  waiting for transfers between devices  204 us (57%)
  blocking collectives  122 us (34%)
  matrix products  14.4 us (4%)
  between operations  14.2 us (4%)
  local copies, waits for them, and re-layouts  5.56 us (2%)
    unnamed x3, waiting for transfers between devices  204 us
    all_gather x1, blocking collectives, on_device(): lax.all_gather(expert_ids, 'dp', axis=0, tiled=True)  49.7 us
    all_gather x1, blocking collectives, on_device(): lax.all_gather(gate_levels, 'dp', axis=0, tiled=True)  41.4 us
    psum x1, blocking collectives, on_device(): moe_out = lax.psum(combined, 'expert').astype(jnp.bfloat16)  30.8 us
    dot_general x1, matrix products, on_device(): jnp.einsum('nrsl,nsld->nrd', weights, outputs, precision=lax.Precision.HI...  7.47 us
  transfers between devices with their start and end apart: 2, of which 1 were waited for; matrix products, arithmetic and copies ran while one was open for 1% of the time, Pallas kernels for 0%

commit v1 on v0

v1 whole, which is shorter than its diff:
```python
import functools

import jax
import jax.numpy as jnp
from jax import lax
from jax.experimental import pallas as pl
from jax.experimental.pallas import tpu as pltpu
from jax.sharding import PartitionSpec as P

NX = 4
MESH = pl.DeviceIdType.MESH
F32 = jnp.float32
BF16 = jnp.bfloat16


def moe_kernel(
    nz, ny, ids, levels, tok, w_gate, w_up, w_down, out,
    wgu, wd, comp, comp_in, mix, mix_in, grid, part, part_in, near, far_in, merged,
    x_in, z_out, z_in, fin, half_out, half_in,
    w_sem, c_s, c_r, zg_s, zg_r, xg_s, xg_r, xf_s, xf_r, pg_s, pg_r, ps_s, ps_r,
    xs_s, xs_r, zs_s, zs_r, y_s, y_r,
):
    dp = lax.axis_index("dp")
    y = lax.axis_index("expert")
    c = lax.rem(dp, 2)
    x = lax.rem(dp // 2, NX)
    z = dp // (2 * NX)
    oc = 1 - c
    half = tok.shape[1] // 2
    hz = nz // 2
    xl, xr, xo = lax.rem(x + NX - 1, NX), lax.rem(x + 1, NX), lax.rem(x + 2, NX)

    def dev(zz, xx, cc):
        return ((zz * NX + xx) * 2 + cc, y)

    partner, left, right = dev(z, x, oc), dev(z, xl, c), dev(z, xr, c)
    z_to = [dev(lax.rem(z + d, nz), x, c) for d in range(nz)]
    y_to = [(dp, lax.rem(y + d, ny)) for d in range(ny)]
    sent = []

    def desc(src, dst, s, r, to):
        return pltpu.make_async_remote_copy(
            src_ref=src, dst_ref=dst, send_sem=s, recv_sem=r, device_id=to, device_id_type=MESH
        )

    def send(src, dst, s, r, to):
        copy = desc(src, dst, s, r, to)
        copy.start()
        sent.append(copy)

    def arrived(dst, s, r, to):
        desc(dst, dst, s, r, to).wait_recv()

    n_own, ff = w_gate.shape[0], w_gate.shape[2]
    loads = []
    for l in range(n_own):
        loads += [
            pltpu.make_async_copy(w_gate.at[l], wgu.at[l, :, pl.ds(0, ff)], w_sem.at[3 * l]),
            pltpu.make_async_copy(w_up.at[l], wgu.at[l, :, pl.ds(ff, ff)], w_sem.at[3 * l + 1]),
            pltpu.make_async_copy(w_down.at[l], wd.at[pl.ds(l * ff, ff)], w_sem.at[3 * l + 2]),
        ]
    for load in loads:
        load.start()

    barrier = pltpu.get_barrier_semaphore()
    peers = [partner, left, right] + z_to[1:] + y_to[1:]
    for peer in peers:
        pl.semaphore_signal(barrier, inc=1, device_id=peer, device_id_type=MESH)

    n_rows = tok.shape[0]
    row = lax.broadcasted_iota(jnp.int32, (8, 128), 0)
    lane = lax.broadcasted_iota(jnp.int32, (8, 128), 1)
    expert_row = 2 * y + row // 4
    here_row = (row % 4) // 2 == c
    slot_row = row % 2
    expert_lane = 2 * (lane // 8) + (lane % 8) // 4
    here_lane = (lane % 4) // 2 == c
    slot_lane = lane % 2
    seen_row = jnp.zeros((8, 128), jnp.int32)
    seen_lane = jnp.zeros((8, 128), jnp.int32)
    weights = jnp.zeros((8, 128), F32)
    tokens = tok[...].astype(F32)
    compact = jnp.zeros((8, 2 * half), F32)
    for t in range(n_rows):
        id0 = jnp.full((8, 128), ids[t, 0], jnp.int32)
        id1 = jnp.full((8, 128), ids[t, 1], jnp.int32)
        lev0 = jnp.full((8, 128), levels[t, 0], jnp.int32).astype(F32)
        lev1 = jnp.full((8, 128), levels[t, 1], jnp.int32).astype(F32)
        hit = (id0 == expert_row) | (id1 == expert_row)
        take = hit & (seen_row == slot_row) & here_row
        seen_row = seen_row + hit.astype(jnp.int32)
        factor = jnp.where(take, 1.0, 0.0).astype(F32)[:, :1]
        compact = compact + factor * tokens[t : t + 1, :]
        hit0, hit1 = id0 == expert_lane, id1 == expert_lane
        hit = hit0 | hit1
        take = hit & (seen_lane == slot_lane) & here_lane & (row == t)
        seen_lane = seen_lane + hit.astype(jnp.int32)
        weights = jnp.where(take, jnp.where(hit0, lev0, lev1) / (lev0 + lev1), weights)
    comp[0] = compact[:, :half].astype(BF16)
    comp[1] = compact[:, half:].astype(BF16)
    mix[...] = weights

    pl.semaphore_wait(barrier, len(peers))

    send(comp.at[oc], comp_in, c_s.at[0], c_r.at[0], partner)
    send(mix, mix_in, c_s.at[1], c_r.at[1], partner)
    arrived(comp_in, c_s.at[0], c_r.at[0], partner)
    grid[c, x, z] = (comp[c].astype(F32) + comp_in[...].astype(F32)).astype(BF16)

    order = sorted(range(nz), key=lambda d: (min(d, nz - d), d))
    z_src = [lax.rem(z + nz - d, nz) for d in range(nz)]
    for d in order[1:]:
        send(grid.at[c, x, z], grid.at[c, x, z], zg_s.at[d], zg_r.at[d], z_to[d])

    def relay(i):
        d = order[i]
        side = i % 2
        src = grid.at[c, (xl, xr)[side], z_src[d]]
        to = (right, left)[side]
        arrived(src, xg_s.at[side, d], xg_r.at[side, d], to)
        send(src, src, xf_s.at[d], xf_r.at[d], to)

    lag = 3
    for i, d in enumerate(order):
        block = grid.at[c, x, z_src[d]]
        if i:
            arrived(block, zg_s.at[d], zg_r.at[d], z_to[d])
        send(block, block, xg_s.at[0, d], xg_r.at[0, d], right)
        send(block, block, xg_s.at[1, d], xg_r.at[1, d], left)
        if i >= lag:
            relay(i - lag)
    send(grid.at[c, x], grid.at[c, x], pg_s.at[0], pg_r.at[0], partner)
    for i in range(max(nz - lag, 0), nz):
        relay(i)

    def swap_in(k, xx):
        send(grid.at[c, xx], grid.at[c, xx], pg_s.at[k], pg_r.at[k], partner)

    for side, xx in ((0, xl), (1, xr)):
        for i, d in enumerate(order):
            if i % 2 != side:
                arrived(
                    grid.at[c, xx, z_src[d]], xg_s.at[side, d], xg_r.at[side, d], (right, left)[side]
                )
        swap_in(1 + side, xx)

    rows = nz * 8
    own_row = (lax.broadcasted_iota(jnp.int32, (rows, ff), 0) % 8) // 4

    def compute(k, xx):
        arrived(grid.at[oc, xx], pg_s.at[k], pg_r.at[k], partner)
        block0 = grid[0, xx].astype(F32).reshape(rows, half).astype(BF16)
        block1 = grid[1, xx].astype(F32).reshape(rows, half).astype(BF16)
        parts = []
        for l in range(n_own):
            both = jnp.dot(block0, wgu[l, :half, :], preferred_element_type=F32)
            both = both + jnp.dot(block1, wgu[l, half:, :], preferred_element_type=F32)
            gate, up = both[:, :ff], both[:, ff:]
            hidden = gate / (1.0 + jnp.exp(-gate)) * up
            parts.append(jnp.where(own_row == l, hidden, 0.0).astype(BF16))
        hidden = jnp.concatenate(parts, axis=1)
        for h in range(2):
            result = jnp.dot(
                hidden, wd[:, h * half : (h + 1) * half], preferred_element_type=F32
            )
            part[k, h] = result.reshape(nz, 8, half).astype(BF16)
        send(part.at[k, oc], part_in.at[k], ps_s.at[k], ps_r.at[k], partner)

    def pair_sum(k):
        arrived(part_in.at[k], ps_s.at[k], ps_r.at[k], partner)
        return part[k, c].astype(F32) + part_in[k].astype(F32)

    for load in loads:
        load.wait()
    compute(0, x)
    for d in order:
        far = grid.at[c, xo, z_src[d]]
        arrived(far, xf_s.at[d], xf_r.at[d], right)
    swap_in(3, xo)
    compute(1, xl)
    compute(2, xr)
    low, high = pl.ds(0, hz), pl.ds(hz, hz)
    near[0] = pair_sum(1).astype(BF16)
    send(near.at[0, low], x_in.at[1, low], xs_s.at[0], xs_r.at[0], left)
    near[1] = pair_sum(2).astype(BF16)
    send(near.at[1, high], x_in.at[0, high], xs_s.at[1], xs_r.at[1], right)
    compute(3, xo)
    near[2] = pair_sum(3).astype(BF16)
    send(near.at[2, low], far_in.at[0], xs_s.at[2], xs_r.at[2], right)
    send(near.at[2, high], far_in.at[1], xs_s.at[3], xs_r.at[3], left)
    total = pair_sum(0)
    arrived(far_in.at[0], xs_s.at[2], xs_r.at[2], right)
    merged[0] = (near[1, :hz].astype(F32) + far_in[0].astype(F32)).astype(BF16)
    send(merged.at[0], x_in.at[0, low], xs_s.at[4], xs_r.at[4], right)
    arrived(far_in.at[1], xs_s.at[3], xs_r.at[3], left)
    merged[1] = (near[0, hz:].astype(F32) + far_in[1].astype(F32)).astype(BF16)
    send(merged.at[1], x_in.at[1, high], xs_s.at[5], xs_r.at[5], left)
    arrived(x_in.at[1, low], xs_s.at[0], xs_r.at[0], left)
    arrived(x_in.at[0, high], xs_s.at[1], xs_r.at[1], right)
    arrived(x_in.at[0, low], xs_s.at[4], xs_r.at[4], right)
    arrived(x_in.at[1, high], xs_s.at[5], xs_r.at[5], left)
    z_out[...] = (total + x_in[0].astype(F32) + x_in[1].astype(F32)).astype(BF16)

    for d in reversed(order[1:]):
        send(z_out.at[lax.rem(z + d, nz)], z_in.at[d], zs_s.at[d], zs_r.at[d], z_to[d])
    final = z_out[z].astype(F32)
    for d in order[1:]:
        arrived(z_in.at[d], zs_s.at[d], zs_r.at[d], z_to[d])
        final = final + z_in[d].astype(F32)

    fin[y] = final.astype(BF16)
    y_order = sorted(range(1, ny), key=lambda d: -min(d, ny - d))
    for d in y_order:
        send(fin.at[y], fin.at[y], y_s.at[d], y_r.at[d], y_to[d])
    arrived(mix_in, c_s.at[1], c_r.at[1], partner)
    for d in reversed(y_order):
        arrived(fin.at[lax.rem(y + ny - d, ny)], y_s.at[d], y_r.at[d], y_to[d])
    values = fin[...].astype(F32).reshape(ny * 8, half)
    other = jnp.dot(
        mix_in[:, : ny * 8], values, precision=lax.Precision.HIGHEST, preferred_element_type=F32
    )
    half_out[...] = other.astype(BF16)
    send(half_out, half_in, c_s.at[2], c_r.at[2], partner)
    mine = jnp.dot(
        mix[:, : ny * 8], values, precision=lax.Precision.HIGHEST, preferred_element_type=F32
    )
    arrived(half_in, c_s.at[2], c_r.at[2], partner)
    theirs = half_in[...].astype(F32)
    out[:, :half] = jnp.where(c == 0, mine, theirs).astype(BF16)
    out[:, half:] = jnp.where(c == 0, theirs, mine).astype(BF16)
    for copy in sent:
        copy.wait_send()


def on_device(nz, ny, tokens, expert_ids, gate_levels, w_gate, w_up, w_down):
    width = tokens.shape[1]
    half = width // 2
    n_own, _, ff = w_gate.shape
    hz = nz // 2
    vmem, smem, dma = pltpu.VMEM, pltpu.SMEM, pltpu.SemaphoreType.DMA
    scratch = [
        vmem((n_own, width, 2 * ff), BF16),
        vmem((n_own * ff, width), BF16),
        vmem((2, 8, half), BF16),
        vmem((8, half), BF16),
        vmem((8, 128), F32),
        vmem((8, 128), F32),
        vmem((2, NX, nz, 8, half), BF16),
        vmem((4, 2, nz, 8, half), BF16),
        vmem((4, nz, 8, half), BF16),
        vmem((3, nz, 8, half), BF16),
        vmem((2, hz, 8, half), BF16),
        vmem((2, hz, 8, half), BF16),
        vmem((2, nz, 8, half), BF16),
        vmem((nz, 8, half), BF16),
        vmem((nz, 8, half), BF16),
        vmem((ny, 8, half), BF16),
        vmem((8, half), BF16),
        vmem((8, half), BF16),
        dma((3 * n_own,)),
        dma((3,)), dma((3,)),
        dma((nz,)), dma((nz,)),
        dma((2, nz)), dma((2, nz)),
        dma((nz,)), dma((nz,)),
        dma((4,)), dma((4,)),
        dma((4,)), dma((4,)),
        dma((6,)), dma((6,)),
        dma((nz,)), dma((nz,)),
        dma((ny,)), dma((ny,)),
    ]
    return pl.pallas_call(
        functools.partial(moe_kernel, nz, ny),
        out_shape=jax.ShapeDtypeStruct(tokens.shape, BF16),
        in_specs=[
            pl.BlockSpec(memory_space=smem),
            pl.BlockSpec(memory_space=smem),
            pl.BlockSpec(memory_space=vmem),
            pl.BlockSpec(memory_space=pl.ANY),
            pl.BlockSpec(memory_space=pl.ANY),
            pl.BlockSpec(memory_space=pl.ANY),
        ],
        out_specs=pl.BlockSpec(memory_space=vmem),
        scratch_shapes=scratch,
        compiler_params=pltpu.CompilerParams(
            collective_id=0, has_side_effects=True, vmem_limit_bytes=40 * 1024 * 1024
        ),
    )(expert_ids, gate_levels, tokens, w_gate, w_up, w_down)


def solution(mesh):
    nz = mesh.shape["dp"] // (2 * NX)
    in_specs = (
        P("dp", None),
        P("dp", None),
        P("dp", None),
        P("expert", None, "dp"),
        P("expert", None, "dp"),
        P("expert", "dp", None),
    )
    return jax.shard_map(
        functools.partial(on_device, nz, mesh.shape["expert"]),
        mesh=mesh, in_specs=in_specs, out_specs=P("dp", None), check_vma=False,
    )
```

time: 361 us -> 62 us (0.17)
  the two profiles are of different devices: /device:TPU:2 before, /device:TPU:1 now
where the time goes in v1:
time: 62 us; the launch traced here: 61.7 us
  Pallas kernels  55.8 us (90%)
  local copies, waits for them, and re-layouts  5.9 us (10%)
    pallas_call x1, Pallas kernels, on_device(): pl.pallas_call(functools.partial(moe_kernel, nz, ny), out_shape=jax.Shape...  55.8 us
    unnamed x13, local copies, waits for them, and re-layouts  5.9 us

profile of v1, /device:TPU:1, one launch (start us, length us, event | category | flops | bytes accessed | tf_op | source)
XLA Modules:
  0.0 61.7 jit_solution(6128077897040128944)
XLA Ops:
  0.0 0.0 copy-start.4
  0.0 0.8 %copy.7.ids = s32[8,2]{1,0:T(8,128)S(1)} copy(s32[8,2]{0,1:T(2,128)} %param.7) | data formatting | bytes 128 | tf_op args[1]
  0.8 0.0 copy-done.4
  0.8 0.1 copy.8.levels
  0.9 0.0 copy-start
  0.9 1.2 %copy-done = bf16[2,2048,128]{2,1,0:T(8,128)(2,1)S(1)} copy-done((bf16[2,2048,128]{2,1,0:T(8,128)(2,1)S(1)}, bf16[2,2048,128]{2,1,0:T(8,128)(2,1)}, u32[]{:S(2)}) %copy-start) | copy-done | bytes 1048600
  2.1 0.0 copy-start.1
  2.1 1.2 %copy-done.1 = bf16[2,2048,128]{2,1,0:T(8,128)(2,1)S(1)} copy-done((bf16[2,2048,128]{2,1,0:T(8,128)(2,1)S(1)}, bf16[2,2048,128]{2,1,0:T(8,128)(2,1)}, u32[]{:S(2)}) %copy-start.1) | copy-done | bytes 1048600
  3.3 0.0 copy-start.2
  3.3 1.2 %copy-done.2 = bf16[2,128,2048]{2,1,0:T(8,128)(2,1)S(1)} copy-done((bf16[2,128,2048]{2,1,0:T(8,128)(2,1)S(1)}, bf16[2,128,2048]{2,1,0:T(8,128)(2,1)}, u32[]{:S(2)}) %copy-start.2) | copy-done | bytes 1048600
  4.5 0.0 copy-start.3
  4.5 0.8 %copy-done.3 = bf16[8,2048]{1,0:T(8,128)(2,1)S(1)} copy-done((bf16[8,2048]{1,0:T(8,128)(2,1)S(1)}, bf16[8,2048]{1,0:T(8,128)(2,1)}, u32[]{:S(2)}) %copy-start.3) | copy-done | bytes 32792
  5.3 55.8 %shard_map.64 = bf16[8,2048]{1,0:T(8,128)(2,1)S(1)} custom-call(s32[8,2]{1,0:T(8,128)S(1)} %copy.7.ids, s32[8,2]{1,0:T(8,128)S(1)} %copy.8.levels, bf16[8,2048]{1,0:T(8,128)(2,1)S(1)} %copy-done.3, bf16[2,2048,128]{2,1,0:T(8,128)(2,1)S(1)} %copy-done, bf16[2,2048,128]{2,1,0:T(8,128)(2,1)S(1)} %copy-done.1, bf16[2,128,2048]{2,1,0:T(8,128)(2,1)S(1)} %copy-done.2), custom_call_target="tpu_custom_call" | custom-call | tf_op jit(solution)/shard_map/pallas_call | solution.py:271
  61.1 0.6 %copy.10 = bf16[8,2048]{1,0:T(8,128)(2,1)} copy(bf16[8,2048]{1,0:T(8,128)(2,1)S(1)} %shard_map.64) | data formatting | bytes 65536
Async XLA Ops:
  0.0 0.8 %copy-start.4 = (s32[8,2]{0,1:T(2,128)S(1)}, s32[8,2]{0,1:T(2,128)}, u32[]{:S(2)}) copy-start(s32[8,2]{0,1:T(2,128)} %param.8) | copy-start | bytes 196
  0.9 1.2 %copy-start = (bf16[2,2048,128]{2,1,0:T(8,128)(2,1)S(1)}, bf16[2,2048,128]{2,1,0:T(8,128)(2,1)}, u32[]{:S(2)}) copy-start(bf16[2,2048,128]{2,1,0:T(8,128)(2,1)} %w_gate.1) | copy-start | bytes 3145732
  2.1 1.2 %copy-start.1 = (bf16[2,2048,128]{2,1,0:T(8,128)(2,1)S(1)}, bf16[2,2048,128]{2,1,0:T(8,128)(2,1)}, u32[]{:S(2)}) copy-start(bf16[2,2048,128]{2,1,0:T(8,128)(2,1)} %w_up.1) | copy-start | bytes 3145732
  3.3 1.2 %copy-start.2 = (bf16[2,128,2048]{2,1,0:T(8,128)(2,1)S(1)}, bf16[2,128,2048]{2,1,0:T(8,128)(2,1)}, u32[]{:S(2)}) copy-start(bf16[2,128,2048]{2,1,0:T(8,128)(2,1)} %w_down.1) | copy-start | bytes 3145732
  4.5 0.8 %copy-start.3 = (bf16[8,2048]{1,0:T(8,128)(2,1)S(1)}, bf16[8,2048]{1,0:T(8,128)(2,1)}, u32[]{:S(2)}) copy-start(bf16[8,2048]{1,0:T(8,128)(2,1)} %tok.1) | copy-start | bytes 98308

commit v2 on v1

v2 whole, which is shorter than its diff:
```python
import functools

import jax
import jax.numpy as jnp
from jax import lax
from jax.experimental import pallas as pl
from jax.experimental.pallas import tpu as pltpu
from jax.sharding import PartitionSpec as P

NX = 4
Q = 2
MESH = pl.DeviceIdType.MESH
F32 = jnp.float32
BF16 = jnp.bfloat16


def moe_kernel(
    nz, ny, ids_hbm, levels_hbm, tok_hbm, w_gate, w_up, w_down, out,
    ids, levels, tok, wgu, wd, comp, comp_in, mix, mix_in, grid, part, part_in, near, far_in, merged,
    x_in, z_out, z_in, fin, half_out, half_in,
    in_sem, w_sem, c_s, c_r, zg_s, zg_r, xg_s, xg_r, xf_s, xf_r, pg_s, pg_r, ps_s, ps_r,
    xs_s, xs_r, zs_s, zs_r, y_s, y_r,
):
    dp = lax.axis_index("dp")
    y = lax.axis_index("expert")
    c = lax.rem(dp, 2)
    x = lax.rem(dp // 2, NX)
    z = dp // (2 * NX)
    oc = 1 - c
    half = tok.shape[1] // 2
    quarter = half // Q
    hz = nz // 2
    xl, xr, xo = lax.rem(x + NX - 1, NX), lax.rem(x + 1, NX), lax.rem(x + 2, NX)

    def dev(zz, xx, cc):
        return ((zz * NX + xx) * 2 + cc, y)

    partner, left, right = dev(z, x, oc), dev(z, xl, c), dev(z, xr, c)
    z_to = [dev(lax.rem(z + d, nz), x, c) for d in range(nz)]
    y_to = [(dp, lax.rem(y + d, ny)) for d in range(ny)]
    sent = []

    def desc(src, dst, s, r, to):
        return pltpu.make_async_remote_copy(
            src_ref=src, dst_ref=dst, send_sem=s, recv_sem=r, device_id=to, device_id_type=MESH
        )

    def send(src, dst, s, r, to):
        copy = desc(src, dst, s, r, to)
        copy.start()
        sent.append(copy)

    def arrived(dst, s, r, to):
        desc(dst, dst, s, r, to).wait_recv()

    small = [
        pltpu.make_async_copy(ids_hbm, ids, in_sem.at[0]),
        pltpu.make_async_copy(levels_hbm, levels, in_sem.at[1]),
        pltpu.make_async_copy(tok_hbm, tok, in_sem.at[2]),
    ]
    for load in small:
        load.start()

    barrier = pltpu.get_barrier_semaphore()
    peers = [partner, left, right] + z_to[1:] + y_to[1:]
    for peer in peers:
        pl.semaphore_signal(barrier, inc=1, device_id=peer, device_id_type=MESH)

    n_own, ff = w_gate.shape[0], w_gate.shape[2]
    loads = []
    for l in range(n_own):
        loads += [
            pltpu.make_async_copy(w_gate.at[l], wgu.at[l, :, pl.ds(0, ff)], w_sem.at[4 * l]),
            pltpu.make_async_copy(w_up.at[l], wgu.at[l, :, pl.ds(ff, ff)], w_sem.at[4 * l + 1]),
        ]
        for h in range(2):
            loads.append(
                pltpu.make_async_copy(
                    w_down.at[l, :, pl.ds(h * half, half)],
                    wd.at[h, pl.ds(l * ff, ff)],
                    w_sem.at[4 * l + 2 + h],
                )
            )
    for load in loads:
        load.start()
    for load in small:
        load.wait()

    n_rows = tok.shape[0]
    row = lax.broadcasted_iota(jnp.int32, (8, 128), 0)
    lane = lax.broadcasted_iota(jnp.int32, (8, 128), 1)
    expert_row = 2 * y + row // 4
    here_row = (row % 4) // 2 == c
    slot_row = row % 2
    expert_lane = 2 * (lane // 8) + (lane % 8) // 4
    here_lane = (lane % 4) // 2 == c
    slot_lane = lane % 2
    seen = jnp.zeros((8, 128), jnp.int32)
    tokens = tok[...].astype(F32)
    compact = jnp.zeros((8, 2 * half), F32)
    for t in range(n_rows):
        id0 = jnp.full((8, 128), ids[0, t], jnp.int32)
        id1 = jnp.full((8, 128), ids[1, t], jnp.int32)
        hit = (id0 == expert_row) | (id1 == expert_row)
        take = hit & (seen == slot_row) & here_row
        seen = seen + hit.astype(jnp.int32)
        factor = jnp.where(take, 1.0, 0.0).astype(F32)[:, :1]
        compact = compact + factor * tokens[t : t + 1, :]
    comp[0] = compact[:, :half].astype(BF16)
    comp[1] = compact[:, half:].astype(BF16)

    pl.semaphore_wait(barrier, len(peers))

    send(comp.at[oc], comp_in, c_s.at[0], c_r.at[0], partner)
    arrived(comp_in, c_s.at[0], c_r.at[0], partner)
    grid[c, x, z] = (comp[c].astype(F32) + comp_in[...].astype(F32)).astype(BF16)

    order = sorted(range(nz), key=lambda d: (min(d, nz - d), d))
    z_src = [lax.rem(z + nz - d, nz) for d in range(nz)]
    for d in order[1:]:
        send(grid.at[c, x, z], grid.at[c, x, z], zg_s.at[d], zg_r.at[d], z_to[d])

    seen = jnp.zeros((8, 128), jnp.int32)
    weights = jnp.zeros((8, 128), F32)
    for t in range(n_rows):
        hit0 = jnp.full((8, 128), ids[0, t], jnp.int32) == expert_lane
        hit1 = jnp.full((8, 128), ids[1, t], jnp.int32) == expert_lane
        lev0 = jnp.full((8, 128), levels[0, t], jnp.int32).astype(F32)
        lev1 = jnp.full((8, 128), levels[1, t], jnp.int32).astype(F32)
        hit = hit0 | hit1
        take = hit & (seen == slot_lane) & here_lane & (row == t)
        seen = seen + hit.astype(jnp.int32)
        weights = jnp.where(take, jnp.where(hit0, lev0, lev1) / (lev0 + lev1), weights)
    mix[...] = weights
    send(mix, mix_in, c_s.at[1], c_r.at[1], partner)

    def relay(i):
        d = order[i]
        side = i % 2
        src = grid.at[c, (xl, xr)[side], z_src[d]]
        to = (right, left)[side]
        arrived(src, xg_s.at[side, d], xg_r.at[side, d], to)
        send(src, src, xf_s.at[d], xf_r.at[d], to)

    lag = 3
    for i, d in enumerate(order):
        block = grid.at[c, x, z_src[d]]
        if i:
            arrived(block, zg_s.at[d], zg_r.at[d], z_to[d])
        send(block, block, xg_s.at[0, d], xg_r.at[0, d], right)
        send(block, block, xg_s.at[1, d], xg_r.at[1, d], left)
        if i >= lag:
            relay(i - lag)
    send(grid.at[c, x], grid.at[c, x], pg_s.at[0], pg_r.at[0], partner)
    for i in range(max(nz - lag, 0), nz):
        relay(i)

    def swap_in(k, xx):
        send(grid.at[c, xx], grid.at[c, xx], pg_s.at[k], pg_r.at[k], partner)

    for side, xx in ((0, xl), (1, xr)):
        for i, d in enumerate(order):
            if i % 2 != side:
                arrived(
                    grid.at[c, xx, z_src[d]], xg_s.at[side, d], xg_r.at[side, d], (right, left)[side]
                )
        swap_in(1 + side, xx)

    rows = nz * 8
    own_row = (lax.broadcasted_iota(jnp.int32, (rows, ff), 0) % 8) // 4

    def compute(k, xx):
        arrived(grid.at[oc, xx], pg_s.at[k], pg_r.at[k], partner)
        block0 = grid[0, xx].astype(F32).reshape(rows, half).astype(BF16)
        block1 = grid[1, xx].astype(F32).reshape(rows, half).astype(BF16)
        parts = []
        for l in range(n_own):
            both = jnp.dot(block0, wgu[l, :half, :], preferred_element_type=F32)
            both = both + jnp.dot(block1, wgu[l, half:, :], preferred_element_type=F32)
            gate, up = both[:, :ff], both[:, ff:]
            hidden = gate / (1.0 + jnp.exp(-gate)) * up
            parts.append(jnp.where(own_row == l, hidden, 0.0).astype(BF16))
        hidden = jnp.concatenate(parts, axis=1)
        for h in (oc, c):
            result = jnp.dot(hidden, wd[h], preferred_element_type=F32).reshape(nz, 8, half)
            for q in range(Q):
                part[k, h, q] = result[:, :, q * quarter : (q + 1) * quarter].astype(BF16)
                if h is oc:
                    send(part.at[k, oc, q], part_in.at[k, q], ps_s.at[k, q], ps_r.at[k, q], partner)

    def pair_sum(k, q):
        arrived(part_in.at[k, q], ps_s.at[k, q], ps_r.at[k, q], partner)
        return part[k, c, q].astype(F32) + part_in[k, q].astype(F32)

    for load in loads:
        load.wait()
    compute(0, x)
    for d in order:
        far = grid.at[c, xo, z_src[d]]
        arrived(far, xf_s.at[d], xf_r.at[d], right)
    swap_in(3, xo)
    compute(1, xl)
    compute(2, xr)

    low, high = pl.ds(0, hz), pl.ds(hz, hz)
    for q in range(Q):
        near[0, q] = pair_sum(1, q).astype(BF16)
        send(near.at[0, q, low], x_in.at[1, q, low], xs_s.at[0, q], xs_r.at[0, q], left)
        near[1, q] = pair_sum(2, q).astype(BF16)
        send(near.at[1, q, high], x_in.at[0, q, high], xs_s.at[1, q], xs_r.at[1, q], right)
    compute(3, xo)
    for q in range(Q):
        near[2, q] = pair_sum(3, q).astype(BF16)
        send(near.at[2, q, low], far_in.at[0, q], xs_s.at[2, q], xs_r.at[2, q], right)
        send(near.at[2, q, high], far_in.at[1, q], xs_s.at[3, q], xs_r.at[3, q], left)
    for q in range(Q):
        arrived(far_in.at[0, q], xs_s.at[2, q], xs_r.at[2, q], right)
        merged[0, q] = (near[1, q, :hz].astype(F32) + far_in[0, q].astype(F32)).astype(BF16)
        send(merged.at[0, q], x_in.at[0, q, low], xs_s.at[4, q], xs_r.at[4, q], right)
        arrived(far_in.at[1, q], xs_s.at[3, q], xs_r.at[3, q], left)
        merged[1, q] = (near[0, q, hz:].astype(F32) + far_in[1, q].astype(F32)).astype(BF16)
        send(merged.at[1, q], x_in.at[1, q, high], xs_s.at[5, q], xs_r.at[5, q], left)

    for q in range(Q):
        total = pair_sum(0, q)
        arrived(x_in.at[1, q, low], xs_s.at[0, q], xs_r.at[0, q], left)
        arrived(x_in.at[0, q, high], xs_s.at[1, q], xs_r.at[1, q], right)
        arrived(x_in.at[0, q, low], xs_s.at[4, q], xs_r.at[4, q], right)
        arrived(x_in.at[1, q, high], xs_s.at[5, q], xs_r.at[5, q], left)
        z_out[q] = (total + x_in[0, q].astype(F32) + x_in[1, q].astype(F32)).astype(BF16)
        for d in reversed(order[1:]):
            send(
                z_out.at[q, lax.rem(z + d, nz)], z_in.at[q, d], zs_s.at[q, d], zs_r.at[q, d], z_to[d]
            )

    y_order = sorted(range(1, ny), key=lambda d: -min(d, ny - d))
    for q in range(Q):
        final = z_out[q, z].astype(F32)
        for d in order[1:]:
            arrived(z_in.at[q, d], zs_s.at[q, d], zs_r.at[q, d], z_to[d])
            final = final + z_in[q, d].astype(F32)
        fin[q, y] = final.astype(BF16)
        for d in y_order:
            send(fin.at[q, y], fin.at[q, y], y_s.at[q, d], y_r.at[q, d], y_to[d])

    arrived(mix_in, c_s.at[1], c_r.at[1], partner)
    gates = jnp.concatenate([mix[...], mix_in[...]], axis=0)
    terms = []
    for _ in range(3):
        term = gates.astype(BF16).astype(F32)
        gates = gates - term
        terms.append(term)
    terms = jnp.concatenate(terms, axis=0)[:, : ny * 8].astype(BF16)
    mine = []
    for q in range(Q):
        for d in reversed(y_order):
            arrived(fin.at[q, lax.rem(y + ny - d, ny)], y_s.at[q, d], y_r.at[q, d], y_to[d])
        values = fin[q].astype(F32).reshape(ny * 8, quarter).astype(BF16)
        mixed = jnp.dot(terms, values, preferred_element_type=F32)
        mixed = mixed[32:] + mixed[16:32] + mixed[:16]
        half_out[q] = mixed[8:].astype(BF16)
        send(half_out.at[q], half_in.at[q], c_s.at[2 + q], c_r.at[2 + q], partner)
        mine.append(mixed[:8])
    for q in range(Q):
        arrived(half_in.at[q], c_s.at[2 + q], c_r.at[2 + q], partner)
        theirs = half_in[q].astype(F32)
        first, second = q * quarter, half + q * quarter
        out[:, first : first + quarter] = jnp.where(c == 0, mine[q], theirs).astype(BF16)
        out[:, second : second + quarter] = jnp.where(c == 0, theirs, mine[q]).astype(BF16)
    for copy in sent:
        copy.wait_send()


def on_device(nz, ny, tokens, expert_ids, gate_levels, w_gate, w_up, w_down):
    width = tokens.shape[1]
    half = width // 2
    n_own, _, ff = w_gate.shape
    hz = nz // 2
    vmem, smem, dma = pltpu.VMEM, pltpu.SMEM, pltpu.SemaphoreType.DMA
    quarter = half // Q
    scratch = [
        smem((2, tokens.shape[0]), jnp.int32),
        smem((2, tokens.shape[0]), jnp.int32),
        vmem(tokens.shape, BF16),
        vmem((n_own, width, 2 * ff), BF16),
        vmem((2, n_own * ff, half), BF16),
        vmem((2, 8, half), BF16),
        vmem((8, half), BF16),
        vmem((8, 128), F32),
        vmem((8, 128), F32),
        vmem((2, NX, nz, 8, half), BF16),
        vmem((4, 2, Q, nz, 8, quarter), BF16),
        vmem((4, Q, nz, 8, quarter), BF16),
        vmem((3, Q, nz, 8, quarter), BF16),
        vmem((2, Q, hz, 8, quarter), BF16),
        vmem((2, Q, hz, 8, quarter), BF16),
        vmem((2, Q, nz, 8, quarter), BF16),
        vmem((Q, nz, 8, quarter), BF16),
        vmem((Q, nz, 8, quarter), BF16),
        vmem((Q, ny, 8, quarter), BF16),
        vmem((Q, 8, quarter), BF16),
        vmem((Q, 8, quarter), BF16),
        dma((3,)),
        dma((4 * n_own,)),
        dma((2 + Q,)), dma((2 + Q,)),
        dma((nz,)), dma((nz,)),
        dma((2, nz)), dma((2, nz)),
        dma((nz,)), dma((nz,)),
        dma((4,)), dma((4,)),
        dma((4, Q)), dma((4, Q)),
        dma((6, Q)), dma((6, Q)),
        dma((Q, nz)), dma((Q, nz)),
        dma((Q, ny)), dma((Q, ny)),
    ]
    return pl.pallas_call(
        functools.partial(moe_kernel, nz, ny),
        out_shape=jax.ShapeDtypeStruct(tokens.shape, BF16),
        in_specs=[pl.BlockSpec(memory_space=pl.ANY)] * 6,
        out_specs=pl.BlockSpec(memory_space=vmem),
        scratch_shapes=scratch,
        compiler_params=pltpu.CompilerParams(
            collective_id=0, has_side_effects=True, vmem_limit_bytes=67043328
        ),
    )(expert_ids.T, gate_levels.T, tokens, w_gate, w_up, w_down)


def solution(mesh):
    nz = mesh.shape["dp"] // (2 * NX)
    in_specs = (
        P("dp", None),
        P("dp", None),
        P("dp", None),
        P("expert", None, "dp"),
        P("expert", None, "dp"),
        P("expert", "dp", None),
    )
    return jax.shard_map(
        functools.partial(on_device, nz, mesh.shape["expert"]),
        mesh=mesh, in_specs=in_specs, out_specs=P("dp", None), check_vma=False,
    )
```

time: 62 us -> 56.1 us (0.905)
  local copies, waits for them, and re-layouts: 5.9 us -> 1.38 us
  Pallas kernels: 55.8 us -> 54.5 us
    unnamed x13 -> x1, local copies, waits for them, and re-layouts: 5.9 us -> 1.38 us
    pallas_call x1, Pallas kernels: 55.8 us -> 54.5 us  [on_device(): pl.pallas_call(functools.partial(moe_kernel, nz, ny), out_shape=jax.Shape...]
where the time goes in v2:
time: 56.1 us; the launch traced here: 55.9 us
  Pallas kernels  54.5 us (97%)
  local copies, waits for them, and re-layouts  1.38 us (2%)
    pallas_call x1, Pallas kernels, on_device(): pl.pallas_call(functools.partial(moe_kernel, nz, ny), out_shape=jax.Shape...  54.5 us
    unnamed x1, local copies, waits for them, and re-layouts  1.38 us

profile of v2, /device:TPU:1, one launch (start us, length us, event | category | flops | bytes accessed | tf_op | source)
XLA Modules:
  0.0 55.9 jit_solution(5070992458165443120)
XLA Ops:
  0.0 54.5 %shard_map.64 = bf16[8,2048]{1,0:T(8,128)(2,1)} custom-call(s32[2,8]{1,0:T(2,128)} %bitcast.2, s32[2,8]{1,0:T(2,128)} %bitcast.3, bf16[8,2048]{1,0:T(8,128)(2,1)} %tok_hbm.1, bf16[2,2048,128]{2,1,0:T(8,128)(2,1)} %w_gate.1, bf16[2,2048,128]{2,1,0:T(8,128)(2,1)} %w_up.1, bf16[2,128,2048]{2,1,0:T(8,128)(2,1)} %w_down.1), custom_call_target="tpu_custom_call" | custom-call | tf_op jit(solution)/shard_map/pallas_call | solution.py:315
  54.6 1.4 %copy.8 = bf16[8,2048]{1,0:T(8,128)(2,1)} copy(bf16[8,2048]{1,0:T(8,128)(2,1)} %shard_map.64) | data formatting | bytes 65536

commit v3 on v2

--- a/solution.py
+++ b/solution.py
@@ -36,6 +36,7 @@
         return ((zz * NX + xx) * 2 + cc, y)
 
     partner, left, right = dev(z, x, oc), dev(z, xl, c), dev(z, xr, c)
+    opposite = dev(z, xo, c)
     z_to = [dev(lax.rem(z + d, nz), x, c) for d in range(nz)]
     y_to = [(dp, lax.rem(y + d, ny)) for d in range(ny)]
     sent = []
@@ -62,7 +63,7 @@
         load.start()
 
     barrier = pltpu.get_barrier_semaphore()
-    peers = [partner, left, right] + z_to[1:] + y_to[1:]
+    peers = [partner, left, right, opposite] + z_to[1:] + y_to[1:]
     for peer in peers:
         pl.semaphore_signal(barrier, inc=1, device_id=peer, device_id_type=MESH)
 
@@ -117,7 +118,7 @@
 
     order = sorted(range(nz), key=lambda d: (min(d, nz - d), d))
     z_src = [lax.rem(z + nz - d, nz) for d in range(nz)]
-    for d in order[1:]:
+    for d in reversed(order[1:]):
         send(grid.at[c, x, z], grid.at[c, x, z], zg_s.at[d], zg_r.at[d], z_to[d])
 
     seen = jnp.zeros((8, 128), jnp.int32)
@@ -143,16 +144,19 @@
         send(src, src, xf_s.at[d], xf_r.at[d], to)
 
     lag = 3
+    n_relay = min(nz, 5)
     for i, d in enumerate(order):
         block = grid.at[c, x, z_src[d]]
         if i:
             arrived(block, zg_s.at[d], zg_r.at[d], z_to[d])
         send(block, block, xg_s.at[0, d], xg_r.at[0, d], right)
         send(block, block, xg_s.at[1, d], xg_r.at[1, d], left)
-        if i >= lag:
+        if i >= n_relay:
+            send(block, block, xf_s.at[d], xf_r.at[d], opposite)
+        if lag <= i < n_relay + lag:
             relay(i - lag)
     send(grid.at[c, x], grid.at[c, x], pg_s.at[0], pg_r.at[0], partner)
-    for i in range(max(nz - lag, 0), nz):
+    for i in range(max(nz - lag, 0), n_relay):
         relay(i)
 
     def swap_in(k, xx):
@@ -160,7 +164,7 @@
 
     for side, xx in ((0, xl), (1, xr)):
         for i, d in enumerate(order):
-            if i % 2 != side:
+            if i % 2 != side or i >= n_relay:
                 arrived(
                     grid.at[c, xx, z_src[d]], xg_s.at[side, d], xg_r.at[side, d], (right, left)[side]
                 )
@@ -170,7 +174,12 @@
     own_row = (lax.broadcasted_iota(jnp.int32, (rows, ff), 0) % 8) // 4
 
     def compute(k, xx):
-        arrived(grid.at[oc, xx], pg_s.at[k], pg_r.at[k], partner)
+        if k == 3:
+            for d in order:
+                far = grid.at[oc, xo, z_src[d]]
+                arrived(far, pg_s.at[3 + d], pg_r.at[3 + d], partner)
+        else:
+            arrived(grid.at[oc, xx], pg_s.at[k], pg_r.at[k], partner)
         block0 = grid[0, xx].astype(F32).reshape(rows, half).astype(BF16)
         block1 = grid[1, xx].astype(F32).reshape(rows, half).astype(BF16)
         parts = []
@@ -198,21 +207,27 @@
     for d in order:
         far = grid.at[c, xo, z_src[d]]
         arrived(far, xf_s.at[d], xf_r.at[d], right)
-    swap_in(3, xo)
+        send(far, far, pg_s.at[3 + d], pg_r.at[3 + d], partner)
     compute(1, xl)
     compute(2, xr)
+    compute(3, xo)
 
     low, high = pl.ds(0, hz), pl.ds(hz, hz)
+    def near_send(q):
+        send(near.at[0, q, low], x_in.at[1, q, low], xs_s.at[0, q], xs_r.at[0, q], left)
+        send(near.at[1, q, high], x_in.at[0, q, high], xs_s.at[1, q], xs_r.at[1, q], right)
+
     for q in range(Q):
         near[0, q] = pair_sum(1, q).astype(BF16)
-        send(near.at[0, q, low], x_in.at[1, q, low], xs_s.at[0, q], xs_r.at[0, q], left)
         near[1, q] = pair_sum(2, q).astype(BF16)
-        send(near.at[1, q, high], x_in.at[0, q, high], xs_s.at[1, q], xs_r.at[1, q], right)
-    compute(3, xo)
+        if q == 0:
+            near_send(q)
     for q in range(Q):
         near[2, q] = pair_sum(3, q).astype(BF16)
         send(near.at[2, q, low], far_in.at[0, q], xs_s.at[2, q], xs_r.at[2, q], right)
         send(near.at[2, q, high], far_in.at[1, q], xs_s.at[3, q], xs_r.at[3, q], left)
+    for q in range(1, Q):
+        near_send(q)
     for q in range(Q):
         arrived(far_in.at[0, q], xs_s.at[2, q], xs_r.at[2, q], right)
         merged[0, q] = (near[1, q, :hz].astype(F32) + far_in[0, q].astype(F32)).astype(BF16)
@@ -306,7 +321,7 @@
         dma((nz,)), dma((nz,)),
         dma((2, nz)), dma((2, nz)),
         dma((nz,)), dma((nz,)),
-        dma((4,)), dma((4,)),
+        dma((3 + nz,)), dma((3 + nz,)),
         dma((4, Q)), dma((4, Q)),
         dma((6, Q)), dma((6, Q)),
         dma((Q, nz)), dma((Q, nz)),

time: 56.1 us -> 56.4 us (level)
  no operation moved by 1% of the time
where the time goes in v3:
time: 56.4 us; the launch traced here: 56.2 us
  Pallas kernels  54.8 us (97%)
  local copies, waits for them, and re-layouts  1.38 us (2%)
    pallas_call x1, Pallas kernels, on_device(): pl.pallas_call(functools.partial(moe_kernel, nz, ny), out_shape=jax.Shape...  54.8 us
    unnamed x1, local copies, waits for them, and re-layouts  1.38 us

profile of v3, /device:TPU:1, one launch (start us, length us, event | category | flops | bytes accessed | tf_op | source)
XLA Modules:
  0.0 56.2 jit_solution(8707119681303905473)
XLA Ops:
  0.0 54.8 %shard_map.64 = bf16[8,2048]{1,0:T(8,128)(2,1)} custom-call(s32[2,8]{1,0:T(2,128)} %bitcast.2, s32[2,8]{1,0:T(2,128)} %bitcast.3, bf16[8,2048]{1,0:T(8,128)(2,1)} %tok_hbm.1, bf16[2,2048,128]{2,1,0:T(8,128)(2,1)} %w_gate.1, bf16[2,2048,128]{2,1,0:T(8,128)(2,1)} %w_up.1, bf16[2,128,2048]{2,1,0:T(8,128)(2,1)} %w_down.1), custom_call_target="tpu_custom_call" | custom-call | tf_op jit(solution)/shard_map/pallas_call | solution.py:330
  54.9 1.4 %copy.8 = bf16[8,2048]{1,0:T(8,128)(2,1)} copy(bf16[8,2048]{1,0:T(8,128)(2,1)} %shard_map.64) | data formatting | bytes 65536

commit v4 on v3

--- a/solution.py
+++ b/solution.py
@@ -50,6 +50,11 @@
         copy = desc(src, dst, s, r, to)
         copy.start()
         sent.append(copy)
+
+    def flush(count):
+        for copy in sent[:count]:
+            copy.wait_send()
+        del sent[:count]
 
     def arrived(dst, s, r, to):
         desc(dst, dst, s, r, to).wait_recv()
@@ -213,6 +218,8 @@
     compute(3, xo)
 
     low, high = pl.ds(0, hz), pl.ds(hz, hz)
+    gathered = len(sent)
+
     def near_send(q):
         send(near.at[0, q, low], x_in.at[1, q, low], xs_s.at[0, q], xs_r.at[0, q], left)
         send(near.at[1, q, high], x_in.at[0, q, high], xs_s.at[1, q], xs_r.at[1, q], right)
@@ -228,6 +235,7 @@
         send(near.at[2, q, high], far_in.at[1, q], xs_s.at[3, q], xs_r.at[3, q], left)
     for q in range(1, Q):
         near_send(q)
+    flush(gathered)
     for q in range(Q):
         arrived(far_in.at[0, q], xs_s.at[2, q], xs_r.at[2, q], right)
         merged[0, q] = (near[1, q, :hz].astype(F32) + far_in[0, q].astype(F32)).astype(BF16)
@@ -236,6 +244,7 @@
         merged[1, q] = (near[0, q, hz:].astype(F32) + far_in[1, q].astype(F32)).astype(BF16)
         send(merged.at[1, q], x_in.at[1, q, high], xs_s.at[5, q], xs_r.at[5, q], left)
 
+    summed = len(sent)
     for q in range(Q):
         total = pair_sum(0, q)
         arrived(x_in.at[1, q, low], xs_s.at[0, q], xs_r.at[0, q], left)
@@ -248,6 +257,8 @@
                 z_out.at[q, lax.rem(z + d, nz)], z_in.at[q, d], zs_s.at[q, d], zs_r.at[q, d], z_to[d]
             )
 
+    flush(summed)
+    shared = len(sent)
     y_order = sorted(range(1, ny), key=lambda d: -min(d, ny - d))
     for q in range(Q):
         final = z_out[q, z].astype(F32)
@@ -258,6 +269,7 @@
         for d in y_order:
             send(fin.at[q, y], fin.at[q, y], y_s.at[q, d], y_r.at[q, d], y_to[d])
 
+    flush(shared)
     arrived(mix_in, c_s.at[1], c_r.at[1], partner)
     gates = jnp.concatenate([mix[...], mix_in[...]], axis=0)
     terms = []
@@ -267,6 +279,7 @@
         terms.append(term)
     terms = jnp.concatenate(terms, axis=0)[:, : ny * 8].astype(BF16)
     mine = []
+    spread = len(sent)
     for q in range(Q):
         for d in reversed(y_order):
             arrived(fin.at[q, lax.rem(y + ny - d, ny)], y_s.at[q, d], y_r.at[q, d], y_to[d])
@@ -276,14 +289,14 @@
         half_out[q] = mixed[8:].astype(BF16)
         send(half_out.at[q], half_in.at[q], c_s.at[2 + q], c_r.at[2 + q], partner)
         mine.append(mixed[:8])
+    flush(spread)
     for q in range(Q):
         arrived(half_in.at[q], c_s.at[2 + q], c_r.at[2 + q], partner)
         theirs = half_in[q].astype(F32)
         first, second = q * quarter, half + q * quarter
         out[:, first : first + quarter] = jnp.where(c == 0, mine[q], theirs).astype(BF16)
         out[:, second : second + quarter] = jnp.where(c == 0, theirs, mine[q]).astype(BF16)
-    for copy in sent:
-        copy.wait_send()
+    flush(len(sent))
 
 
 def on_device(nz, ny, tokens, expert_ids, gate_levels, w_gate, w_up, w_down):

time: 56.4 us -> 56.3 us (level)
  no operation moved by 1% of the time
where the time goes in v4:
time: 56.3 us; the launch traced here: 56.1 us
  Pallas kernels  54.7 us (97%)
  local copies, waits for them, and re-layouts  1.38 us (2%)
    pallas_call x1, Pallas kernels, on_device(): pl.pallas_call(functools.partial(moe_kernel, nz, ny), out_shape=jax.Shape...  54.7 us
    unnamed x1, local copies, waits for them, and re-layouts  1.38 us

profile of v4, /device:TPU:1, one launch (start us, length us, event | category | flops | bytes accessed | tf_op | source)
XLA Modules:
  0.0 56.1 jit_solution(6434841310262599018)
XLA Ops:
  0.0 54.7 %shard_map.64 = bf16[8,2048]{1,0:T(8,128)(2,1)} custom-call(s32[2,8]{1,0:T(2,128)} %bitcast.2, s32[2,8]{1,0:T(2,128)} %bitcast.3, bf16[8,2048]{1,0:T(8,128)(2,1)} %tok_hbm.1, bf16[2,2048,128]{2,1,0:T(8,128)(2,1)} %w_gate.1, bf16[2,2048,128]{2,1,0:T(8,128)(2,1)} %w_up.1, bf16[2,128,2048]{2,1,0:T(8,128)(2,1)} %w_down.1), custom_call_target="tpu_custom_call" | custom-call | tf_op jit(solution)/shard_map/pallas_call | solution.py:343
  54.7 1.4 %copy.8 = bf16[8,2048]{1,0:T(8,128)(2,1)} copy(bf16[8,2048]{1,0:T(8,128)(2,1)} %shard_map.64) | data formatting | bytes 65536
